TPU v7x, 32 devices: a whole 2x2x4 slice. The times are simulated.
32 devices in a mesh: seq: 8 (over y, x, core), req: 4 (over z).
Axes of the slice: x: 2, y: 2, z: 4, core: 2. Of those that a mesh axis runs over, the one named last changes fastest.
Arguments:
- queries: bfloat16 [8, 256, 1536], P('req', 'seq'), as said below
- new_kv: bfloat16 [2, 8, 256, 512], P(None, 'req', 'seq'), may hold values from -6 to 6
- cache_kv: bfloat16 [2, 8, 2048, 512], P(None, 'req', 'seq'), as said below
- cache_spans: int32 [8, 2], P('req'), may hold values from 0 to 2048, as said below
- recompute_rows: int32 [8, 256], P('req'), may hold values from 0 to 2047, as said below
- held_states: bfloat16 [8, 256, 1536], P('req', 'seq'), may hold values from -6 to 6
- key_weight: bfloat16 [1536, 512], replicated, may hold values from -0.15625 to 0.15625
- norm_gain: float32 [1536], replicated, may hold values from 0.1 to 1.9
- routes: int32 [8, 256, 8], P('req', 'seq'), may hold values from 0 to 19, all different within a row; in each aligned block of 32 rows (0 to 31, 32 to 63, ..., all dimensions but the last counted through in order) at most 16 rows name the same one
- route_weights: float32 [8, 256, 8], P('req', 'seq'), may hold values from 0.05 to 1
- expert_gate_up: bfloat16 [20, 1536, 1024], P('req'), may hold values from -0.15625 to 0.15625
- expert_down: bfloat16 [20, 512, 1536], P('req'), may hold values from -0.25 to 0.25
Outputs:
- layer_out: bfloat16 [8, 256, 1536], P('req', 'seq')
Inputs may be any that keep to these rules, and one draw needn't show every extreme that they name: `routes`: in each aligned block of 32 rows of one request (one device's rows of that request) no expert is named more than 16 times. cache_spans[r] = (start, length): 1024 <= length <= 2048 with some request of length 2048; 0 <= start <= 512 with some request starting at 0. `recompute_rows`: within a request the rows are distinct and lie between the request's start and length. `queries`: entries lie within -6 to 6. `cache_kv`: entries lie within -6 to 6.
All inputs are finite; a program needn't handle non-finite values.
Results may differ from a plain program's by a relative error of at most 0.034.
Values may be sent and summed in bfloat16 or wider, within the bound.
A program may use at most 192 MiB of HBM per device.

v0:
```python
import jax
import jax.numpy as jnp
from jax import lax
from jax.sharding import PartitionSpec as P

H = 24
KVH = 8
HD = 64
FF = 512
TOP = 8
CAP = 16


NEG = -1e30
THETA = 10000.0


def rotate(key_heads, positions):
    half_dim = key_heads.shape[-1] // 2
    exponent = jnp.arange(half_dim).astype(jnp.float32) * (2.0 / key_heads.shape[-1])
    inverse = THETA ** (-exponent)
    angles = positions.astype(jnp.float32)[..., None] * inverse
    cosine = jnp.cos(angles)[..., None, :]
    sine_part = jnp.sin(angles)[..., None, :]
    lower_half = key_heads[..., :half_dim]
    upper_half = key_heads[..., half_dim:]
    return jnp.concatenate(
        [
            lower_half * cosine - upper_half * sine_part,
            upper_half * cosine + lower_half * sine_part,
        ],
        axis=-1,
    )


def partial_attend(packed):
    query_rows, key_rows, value_rows, allowed = packed
    query_count, model_width = query_rows.shape
    key_count = key_rows.shape[0]
    groups = H // KVH
    query_heads = query_rows.reshape(query_count, KVH, groups, HD)
    key_heads = key_rows.reshape(key_count, KVH, HD)
    value_heads = value_rows.reshape(key_count, KVH, HD)
    scores = jnp.einsum(
        "qkgd,nkd->kgqn", query_heads, key_heads, preferred_element_type=jnp.float32
    ) * HD ** (-0.5)
    scores = jnp.where(allowed[None, None, :, :], scores, NEG)
    highest = jnp.max(scores, axis=-1, keepdims=True)
    exps = jnp.exp(scores - highest)
    totals = jnp.sum(exps, axis=-1)
    weights = exps.astype(jnp.bfloat16)
    mixed_rows = jnp.einsum(
        "kgqn,nkd->qkgd", weights, value_heads, preferred_element_type=jnp.float32
    )
    mixed_rows = mixed_rows / jnp.transpose(totals, (2, 0, 1))[..., None]
    log_total = highest[..., 0] + jnp.log(totals)
    log_rows = jnp.transpose(log_total, (2, 0, 1)).reshape(query_count, H)
    return (mixed_rows.reshape(query_count, model_width), log_rows)


def body(
    queries,
    new_kv,
    cache_kv,
    cache_spans,
    recompute_rows,
    held_states,
    key_weight,
    norm_gain,
    routes,
    route_weights,
    expert_gate_up,
    expert_down,
):
    seq_index = lax.axis_index("seq")
    seq_count = lax.axis_size("seq")
    owner_count = lax.axis_size("req")
    req_rows, tok_rows, model_width = queries.shape
    cache_rows = cache_kv.shape[2]
    held_rows = held_states.shape[1]
    local_experts = expert_gate_up.shape[0]
    expert_total = owner_count * local_experts
    my_positions = lax.dynamic_slice_in_dim(recompute_rows, seq_index * held_rows, held_rows, 1)
    projected = jnp.dot(
        held_states.reshape(req_rows * held_rows, model_width),
        key_weight,
        preferred_element_type=jnp.float32,
    )
    rotated = rotate(projected.reshape(req_rows, held_rows, KVH, HD), my_positions)
    rotated = rotated.reshape(req_rows, held_rows, KVH * HD).astype(jnp.bfloat16)
    fresh_rows = lax.all_gather(rotated, "seq", axis=1, tiled=True)
    cache_positions = seq_index * cache_rows + jnp.arange(cache_rows)
    hit_table = recompute_rows[:, None, :] == cache_positions[None, :, None]
    placed = jnp.einsum(
        "rcm,rmk->rck",
        hit_table.astype(jnp.bfloat16),
        fresh_rows,
        preferred_element_type=jnp.float32,
    ).astype(jnp.bfloat16)
    cache_keys = jnp.where(jnp.any(hit_table, axis=2)[:, :, None], placed, cache_kv[0])
    span_start = cache_spans[:, 0:1]
    span_end = cache_spans[:, 1:2]
    all_queries = lax.all_gather(queries, "seq", axis=1, tiled=True)
    step_total = all_queries.shape[1]
    cache_allowed = (cache_positions[None, :] >= span_start) & (cache_positions[None, :] < span_end)
    key_positions = seq_index * tok_rows + jnp.arange(tok_rows)
    step_allowed = key_positions[None, :] <= jnp.arange(step_total)[:, None]
    allowed = jnp.concatenate(
        [
            jnp.broadcast_to(cache_allowed[:, None, :], (req_rows, step_total, cache_rows)),
            jnp.broadcast_to(step_allowed[None], (req_rows, step_total, tok_rows)),
        ],
        axis=2,
    )
    key_rows = jnp.concatenate([cache_keys, new_kv[0]], axis=1)
    value_rows = jnp.concatenate([cache_kv[1], new_kv[1]], axis=1)
    part_out, part_log = lax.map(partial_attend, (all_queries, key_rows, value_rows, allowed))
    piece_out, piece_log = (
        lax.all_to_all(part_out[None], "seq", split_axis=2, concat_axis=0, tiled=True),
        lax.all_to_all(part_log[None], "seq", split_axis=2, concat_axis=0, tiled=True),
    )
    best_log = jnp.max(piece_log, axis=0)
    factors = jnp.exp(piece_log - best_log[None])
    factor_sum = jnp.sum(factors, axis=0)
    spread_out = piece_out.reshape(seq_count, req_rows, tok_rows, H, HD)
    combined = jnp.sum(spread_out * factors[..., None], axis=0) / factor_sum[..., None]
    attended_f = combined.reshape(req_rows, tok_rows, model_width)
    attended = attended_f.astype(jnp.bfloat16)
    attended_f = attended.astype(jnp.float32)
    mean_square = jnp.mean(attended_f * attended_f, axis=-1, keepdims=True)
    normed = (attended_f * lax.rsqrt(mean_square + 1e-06) * norm_gain).astype(jnp.bfloat16)
    route_flat = routes.reshape(req_rows, tok_rows * TOP)
    expert_match = (route_flat[:, :, None] == jnp.arange(expert_total)[None, None, :]).astype(
        jnp.int32
    )
    earlier = jnp.cumsum(expert_match, axis=1) - expert_match
    slot_index = jnp.sum(earlier * expert_match, axis=2)
    target = route_flat * CAP + slot_index
    slot_match = target[:, :, None] == jnp.arange(expert_total * CAP)[None, None, :]
    dispatch = jnp.any(
        slot_match.reshape(req_rows, tok_rows, TOP, expert_total * CAP), axis=2
    ).astype(jnp.bfloat16)
    dispatch = dispatch.reshape(req_rows, tok_rows, owner_count, local_experts, CAP)
    outgoing = jnp.einsum(
        "rtnec,rtd->nrecd", dispatch, normed, preferred_element_type=jnp.float32
    ).astype(jnp.bfloat16)
    hidden = jnp.einsum(
        "srecd,edf->srecf",
        lax.all_to_all(outgoing, "req", split_axis=0, concat_axis=0, tiled=True),
        expert_gate_up,
        preferred_element_type=jnp.float32,
    )
    active = (jax.nn.silu(hidden[..., :FF]) * hidden[..., FF:]).astype(jnp.bfloat16)
    result = jnp.einsum(
        "srecf,efd->srecd", active, expert_down, preferred_element_type=jnp.float32
    ).astype(jnp.bfloat16)
    returned = lax.all_to_all(result, "req", split_axis=0, concat_axis=0, tiled=True)
    owner_of = route_flat // local_experts
    local_of = route_flat % local_experts
    flat_index = (
        (owner_of * req_rows + jnp.arange(req_rows)[:, None]) * local_experts + local_of
    ) * CAP + slot_index
    returned_rows = jnp.take(returned.reshape(-1, model_width), flat_index.reshape(-1), axis=0)
    returned_rows = returned_rows.reshape(req_rows, tok_rows, TOP, model_width)
    mixture = jnp.einsum(
        "rtk,rtkd->rtd",
        route_weights,
        returned_rows.astype(jnp.float32),
        precision=lax.Precision.HIGHEST,
    )
    return (attended_f + mixture).astype(jnp.bfloat16)


def solution(mesh):
    in_specs = (
        P("req", "seq", None),
        P(None, "req", "seq", None),
        P(None, "req", "seq", None),
        P("req", None),
        P("req", None),
        P("req", "seq", None),
        P(),
        P(),
        P("req", "seq", None),
        P("req", "seq", None),
        P("req", None, None),
        P("req", None, None),
    )
    out_specs = P("req", "seq", None)
    return jax.shard_map(body, mesh=mesh, in_specs=in_specs, out_specs=out_specs, check_vma=False)
```

profile of v0, /device:TPU:2, one launch (start us, length us, event | category | flops | bytes accessed | tf_op | source)
XLA Modules:
  0.0 298.9 jit_solution(2745684699913608374)
XLA Ops:
  6.5 1.8 copy.65
  8.4 0.8 dynamic-slice_convert_fusion
  9.2 1.7 copy.63
  11.1 0.9 fusion.47
  12.7 0.3 slice-done
  13.4 10.8 %all_gather.6 = bf16[2,256,512]{2,1,0:T(8,128)(2,1)S(1)} all-gather(bf16[2,32,512]{2,1,0:T(8,128)(2,1)S(1)} %convert_element_type.67), channel_id=1, replica_groups=mesh['seq'=8,'req'=4] {'seq'}, dimensions={1}, use_global_device_ids=true | all-gather | bytes 589824 | tf_op jit(solution)/shard_map/all_gather | solution.py:91
  24.6 0.2 compare_reduce_fusion
  24.8 0.4 fusion.31
  25.2 0.9 pad_maximum_fusion.1
  26.1 1.0 pad_maximum_fusion
  27.1 10.3 %all-gather.2.cloned.1.call-done = bf16[2,256,1536]{2,0,1:T(2,128)(2,1)} async-done(((bf16[2,32,1536]{2,0,1:T(2,128)(2,1)}), bf16[2,256,1536]{2,0,1:T(2,128)(2,1)}) %all-gather.2.cloned.1.call-update) | async-done | bytes 1572880 | tf_op jit(solution)/shard_map/all_gather | solution.py:103
  37.4 4.9 %copy.67 = bf16[2,256,1536]{1,2,0:T(8,128)(2,1)} copy(bf16[2,256,1536]{2,0,1:T(2,128)(2,1)} %all-gather.2.cloned.1.call-done) | data formatting | bytes 3145728 | tf_op jit(solution)/shard_map/while | solution.py:117
  42.3 78.1 %while.12 = (s32[]{:T(128)}, f32[2,256,1536]{2,0,1:T(2,128)}, f32[2,256,24]{1,2,0:T(8,128)S(1)}, bf16[2,288,512]{1,2,0:T(8,128)(2,1)}, pred[2,256,288]{1,2,0:T(8...) while((s32[]{:T(128)}, f32[2,256,1536]{2,0,1:T(2,128)}, ...), condition=%wide.region_4.5_spmd, body=%wide.region_1.4_spmd.sunk | while | flops 472836096 | bytes 62791824 | solution.py:117
  42.3 1.2 constant_dynamic-slice_fusion.8
  43.5 1.0 constant_dynamic-slice_fusion.7
  44.5 0.2 copy.113
  44.7 1.2 fusion.81
  45.9 1.5 fusion.82
  47.4 1.4 copy-done.2
  48.8 1.0 constant_dynamic-slice_fusion.6
  49.9 4.8 %bitcast_divide_fusion.2 = f32[256,8,3,64]{0,3,2,1:T(8,128)S(1)} fusion(bf16[288,8,64,1]{0,2,3,1:T(8,128)(2,1)S(1)} %bitcast.165, f32[8,288,256,3]{2,1,3,0:T(8,128)} %copy-done.2, f32[8,3,256]{2,1,0:T(4,128)S(1)} %get-tuple-element.152, pred[256,288]{0,1:T(8,128)(4,1)S(1)} %dynamic-slice_bitcast_fusion.2, f32[256,8,3]{0,2,1:T(4,128)S(1)} %bitcast.167), kind=kOutput, calls=%fused_computation.8.clone.1 | convolution fusion | flops 233963520 | bytes 9068544 | tf_op jit(solution)/shard_map/while/body/eval_jaxpr/kgqn,nkd->qkgd/dot_general | solution.py:52
  54.7 1.2 copy.114
  55.9 25.4 %dynamic_update_slice.12 = f32[2,256,1536]{2,0,1:T(2,128)} dynamic-update-slice(f32[2,256,1536]{2,0,1:T(2,128)} %get-tuple-element.163, f32[1,256,1536]{2,0,1:T(1,128)S(1)} %copy.114, s32[]{:T(128)} %get-tuple-element.162, s32[]{:T(128)} %constant.54.clone.1..sunk, s32[]{:T(128)} %constant.54.clone.1..sunk) | dynamic-update-slice | bytes 3145732 | tf_op jit(solution)/shard_map/while/body/jit(dynamic_update_index_in_dim)/dynamic_update_slice | solution.py:117
  81.3 1.2 constant_dynamic-slice_fusion.8
  82.5 1.0 constant_dynamic-slice_fusion.7
  83.7 1.2 fusion.81
  84.9 1.5 fusion.82
  86.4 1.4 copy-done.2
  87.9 1.0 constant_dynamic-slice_fusion.6
  88.9 4.8 %bitcast_divide_fusion.2 = f32[256,8,3,64]{0,3,2,1:T(8,128)S(1)} fusion(bf16[288,8,64,1]{0,2,3,1:T(8,128)(2,1)S(1)} %bitcast.165, f32[8,288,256,3]{2,1,3,0:T(8,128)} %copy-done.2, f32[8,3,256]{2,1,0:T(4,128)S(1)} %get-tuple-element.152, pred[256,288]{0,1:T(8,128)(4,1)S(1)} %dynamic-slice_bitcast_fusion.2, f32[256,8,3]{0,2,1:T(4,128)S(1)} %bitcast.167), kind=kOutput, calls=%fused_computation.8.clone.1 | convolution fusion | flops 233963520 | bytes 9068544 | tf_op jit(solution)/shard_map/while/body/eval_jaxpr/kgqn,nkd->qkgd/dot_general | solution.py:52
  93.7 1.2 copy.114
  94.9 25.4 %dynamic_update_slice.12 = f32[2,256,1536]{2,0,1:T(2,128)} dynamic-update-slice(f32[2,256,1536]{2,0,1:T(2,128)} %get-tuple-element.163, f32[1,256,1536]{2,0,1:T(1,128)S(1)} %copy.114, s32[]{:T(128)} %get-tuple-element.162, s32[]{:T(128)} %constant.54.clone.1..sunk, s32[]{:T(128)} %constant.54.clone.1..sunk) | dynamic-update-slice | bytes 3145732 | tf_op jit(solution)/shard_map/while/body/jit(dynamic_update_index_in_dim)/dynamic_update_slice | solution.py:117
  120.5 0.4 reshape.329
  120.9 6.6 %all_to_all.43 = f32[8,1,1536]{2,1,0:T(1,128)S(1)} all-to-all(f32[8,1,1536]{2,1,0:T(1,128)S(1)} %reshape.329), channel_id=1, replica_groups=mesh['seq'=8,'req'=4] {'seq'}, dimensions={0} | all-to-all | bytes 98304 | tf_op jit(solution)/shard_map/all_to_all | solution.py:120
  127.5 5.2 %all-to-all-start = ((f32[1,2,256,1536]{3,1,0,2:T(2,128)}), f32[1,2,256,1536]{3,1,0,2:T(2,128)S(1)}, u32[]{:S(2)}, u32[]{:S(2)}) async-start(f32[1,2,256,1536]{3,1,0,2:T(2,128)} %bitcast.168), calls=%async_computation | async-start | bytes 6291456 | tf_op jit(solution)/shard_map/all_to_all | solution.py:119
  132.9 1.2 reduce-window.6
  134.1 0.2 slice_reduce_fusion
  134.7 0.3 fusion.33
  135.3 0.5 broadcast.314
  135.8 0.8 reduce.12
  136.5 1.2 reshape.330
  137.7 1.1 copy.71
  138.9 1.3 fusion.63
  140.2 1.8 copy.72
  142.0 4.9 %mul.189 = f32[8,2,32,24,64]{4,3,2,0,1:T(8,128)} broadcast(f32[8,2,32,24]{3,2,0,1:T(8,128)} %copy.72), dimensions={0,1,2,3} | broadcast | bytes 3194880 | tf_op jit(solution)/shard_map/mul | solution.py:126
  146.9 6.2 %mul.190 = f32[8,1,2,32,1536]{4,3,0,2,1:T(8,128)} reshape(f32[8,2,32,24,64]{4,3,2,0,1:T(8,128)} %mul.189) | data formatting | bytes 6291456 | tf_op jit(solution)/shard_map/mul | solution.py:126
  153.2 1.2 div.53
  154.3 2.1 div.54
  156.4 12.6 %all-to-all-done = f32[1,2,256,1536]{3,1,0,2:T(2,128)S(1)} async-done(((f32[1,2,256,1536]{3,1,0,2:T(2,128)}), f32[1,2,256,1536]{3,1,0,2:T(2,128)S(1)}, u32[]{:S(2)}, u32[]{:S(2)}) %all-to-all-start) | async-done | bytes 3145760 | tf_op jit(solution)/shard_map/all_to_all | solution.py:119
  169.0 0.6 copy.69
  169.7 1.3 copy-done.3
  170.9 0.7 multiply_reduce_fusion
  171.7 0.3 copy-done.5
  172.1 0.7 fusion.17
  173.0 50.3 %all_to_all.44 = bf16[4,2,5,16,1536]{4,3,1,2,0:T(8,128)(2,1)S(1)} all-to-all(bf16[4,2,5,16,1536]{4,3,1,2,0:T(8,128)(2,1)S(1)} %copy.83), channel_id=1, replica_groups=mesh['seq'=8,'req'=4] {'req'}, dimensions={0} | all-to-all | bytes 3932160 | tf_op jit(solution)/shard_map/all_to_all | solution.py:149
  223.3 8.1 %fusion.22 = f32[4,2,5,16,1024]{4,3,1,0,2:T(8,128)S(1)} fusion(bf16[5,1536,1024]{2,1,0:T(8,128)(2,1)} %param.24, bf16[4,2,5,16,1536]{4,3,1,2,0:T(8,128)(2,1)S(1)} %all_to_all.44), kind=kOutput, calls=%fused_computation.27 | convolution fusion | flops 2013265920 | bytes 20316160 | tf_op jit(solution)/shard_map/srecd,edf->srecf/dot_general | solution.py:147
  231.4 1.4 fusion.18
  232.8 1.4 copy.85
  234.2 4.5 %all-to-all-start.3 = ((bf16[4,2,5,16,1536]{4,3,1,2,0:T(8,128)(2,1)}), bf16[4,2,5,16,1536]{4,3,1,2,0:T(8,128)(2,1)}, u32[]{:S(2)}, u32[]{:S(2)}) async-start(bf16[4,2,5,16,1536]{4,3,1,2,0:T(8,128)(2,1)} %copy.85), calls=%async_computation.3 | async-start | bytes 3932160 | tf_op jit(solution)/shard_map/all_to_all | solution.py:157
  239.3 44.5 %all-to-all-done.3 = bf16[4,2,5,16,1536]{4,3,1,2,0:T(8,128)(2,1)} async-done(((bf16[4,2,5,16,1536]{4,3,1,2,0:T(8,128)(2,1)}), bf16[4,2,5,16,1536]{4,3,1,2,0:T(8,128)(2,1)}, u32[]{:S(2)}, u32[]{:S(2)}) %all-to-all-start.3) | async-done | bytes 1966112 | tf_op jit(solution)/shard_map/all_to_all | solution.py:157
  283.8 1.7 copy.86
  285.5 3.0 gather_fusion
  288.4 2.9 fusion.27
  291.3 0.7 fusion.40
  (94 shorter events, 3.8 us)
Async XLA Ops:
  6.5 4.6 %copy-start = (bf16[2,32,1536]{2,1,0:T(8,128)(2,1)S(1)}, bf16[2,32,1536]{2,1,0:T(8,128)(2,1)}, u32[]{:S(2)}) copy-start(bf16[2,32,1536]{2,1,0:T(8,128)(2,1)} %param.19) | copy-start | bytes 589828
  6.5 30.8 %all-gather.2.cloned.1.call-start = ((), (), s32[]{:S(2)}) async-start(), calls=%async_computation.4 | async-start | bytes 1769472 | tf_op jit(solution)/shard_map/all_gather | solution.py:103
  10.9 1.6 copy-start.6
  12.0 1.0 slice-start
  12.1 1.1 copy-start.14
  12.3 12.3 %copy-start.13 = (s32[2,256]{1,0:T(2,128)S(1)}, s32[2,256]{1,0:T(2,128)}, u32[]{:S(2)}) copy-start(s32[2,256]{1,0:T(2,128)} %param.18) | copy-start | bytes 6148
  12.4 12.5 %copy-start.4 = (bf16[2,2,256,512]{3,2,1,0:T(8,128)(2,1)S(1)}, bf16[2,2,256,512]{3,2,1,0:T(8,128)(2,1)}, u32[]{:S(2)}) copy-start(bf16[2,2,256,512]{3,2,1,0:T(8,128)(2,1)} %param.16) | copy-start | bytes 3145732
  45.9 2.9 copy-start.2
  84.9 2.9 copy-start.2
  127.5 5.2 %copy-start.11 = (s32[2,32,8]{1,2,0:T(8,128)S(1)}, s32[2,32,8]{1,2,0:T(8,128)}, u32[]{:S(2)}) copy-start(s32[2,32,8]{1,2,0:T(8,128)} %param.22) | copy-start | bytes 6148
  127.5 41.5 %all-to-all-start = ((f32[1,2,256,1536]{3,1,0,2:T(2,128)}), f32[1,2,256,1536]{3,1,0,2:T(2,128)S(1)}, u32[]{:S(2)}, u32[]{:S(2)}) async-start(f32[1,2,256,1536]{3,1,0,2:T(2,128)} %bitcast.168), calls=%async_computation | async-start | bytes 6291456 | tf_op jit(solution)/shard_map/all_to_all | solution.py:119
  134.6 0.7 copy-start.8
  146.9 6.2 %copy-start.7 = (f32[2,32,24]{1,2,0:T(8,128)S(1)}, f32[2,32,24]{1,2,0:T(8,128)}, u32[]{:S(2)}) copy-start(f32[2,32,24]{1,2,0:T(8,128)} %get-tuple-element.93) | copy-start | bytes 18436
  169.0 1.9 copy-start.3
  170.9 1.0 copy-start.5
  170.9 1.1 copy-start.10
  173.0 58.4 %slice-start.1 = ((s8[7864320]{0:T(1024)(128)(4,1)}), s8[4194304]{0:T(1024)(128)(4,1)S(1)}, s32[]{:S(2)}) async-start(s8[7864320]{0:T(1024)(128)(4,1)} %bitcast.179), calls=%async_computation.6 | async-start | bytes 8388608
  223.3 8.1 %slice-start.2 = ((s8[7864320]{0:T(1024)(128)(4,1)}), s8[3670016]{0:T(1024)(128)(4,1)S(1)}, s32[]{:S(2)}) async-start(s8[7864320]{0:T(1024)(128)(4,1)} %bitcast.179), calls=%async_computation.7 | async-start | bytes 7340032
  234.2 4.9 %copy-start.9 = (s32[2,256]{1,0:T(2,128)S(1)}, s32[2,256]{1,0:T(2,128)}, u32[]{:S(2)}) copy-start(s32[2,256]{1,0:T(2,128)} %copy-done.8) | copy-start | bytes 6148
  234.2 4.9 %copy-start.12 = (f32[2,32,8]{1,2,0:T(8,128)S(1)}, f32[2,32,8]{1,2,0:T(8,128)}, u32[]{:S(2)}) copy-start(f32[2,32,8]{1,2,0:T(8,128)} %param.23) | copy-start | bytes 6148
  234.2 49.5 %all-to-all-start.3 = ((bf16[4,2,5,16,1536]{4,3,1,2,0:T(8,128)(2,1)}), bf16[4,2,5,16,1536]{4,3,1,2,0:T(8,128)(2,1)}, u32[]{:S(2)}, u32[]{:S(2)}) async-start(bf16[4,2,5,16,1536]{4,3,1,2,0:T(8,128)(2,1)} %copy.85), calls=%async_computation.3 | async-start | bytes 3932160 | tf_op jit(solution)/shard_map/all_to_all | solution.py:157
  285.4 6.6 %copy-start.1 = (bf16[2,32,1536]{2,1,0:T(8,128)(2,1)S(1)}, bf16[2,32,1536]{2,1,0:T(8,128)(2,1)}, u32[]{:S(2)}) copy-start(bf16[2,32,1536]{2,1,0:T(8,128)(2,1)} %param.19) | copy-start | bytes 589828
Sparse Core Ops, SparseCore 0:
  9.2 28.0 all-gather.1
where the time goes:
time: 303 us; the launch traced here: 299 us
  local copies, waits for them, and re-layouts  102 us (34%)
  blocking collectives  67.7 us (22%)
  waiting for transfers between devices  67.4 us (22%)
  matrix products  26.3 us (9%)
  between operations  13.9 us (5%)
  other arithmetic  12 us (4%)
  starting transfers between devices  9.69 us (3%)
    dynamic_update_slice x6, local copies, waits for them, and re-layouts, body(): lax.map(partial_attend, (all_queries, key_rows, value_rows, allowed))  53.2 us
    all_to_all x1, blocking collectives, body(): lax.all_to_all(outgoing, 'req', split_axis=0, concat_axis=0, tiled=True)  50.3 us
    all_to_all x1, waiting for transfers between devices, body(): lax.all_to_all(result, 'req', split_axis=0, concat_axis=0, tiled=True)  44.5 us
    all_to_all x1, waiting for transfers between devices, body(): lax.all_to_all(part_out[None], 'seq', split_axis=2, concat_axis=0, tiled=...  12.6 us
    mul x2, local copies, waits for them, and re-layouts, body(): spread_out * factors[..., None]  11.1 us
    all_gather x1, blocking collectives, body(): fresh_rows = lax.all_gather(rotated, 'seq', axis=1, tiled=True)  10.8 us
    all_gather x1, waiting for transfers between devices, body(): all_queries = lax.all_gather(queries, 'seq', axis=1, tiled=True)  10.3 us
    dot_general x2, matrix products, partial_attend(): jnp.einsum('kgqn,nkd->qkgd', weights, value_heads, preferred_element_type...  9.64 us
  transfers between devices with their start and end apart: 3, of which 3 were waited for; matrix products, arithmetic and copies ran while one was open for 11% of the time, Pallas kernels for 0%

commit v1 on v0

--- a/solution.py
+++ b/solution.py
@@ -58,7 +58,7 @@
     return (mixed_rows.reshape(query_count, model_width), log_rows)
 
 
-def body(
+def body_wide(
     queries,
     new_kv,
     cache_kv,
@@ -171,7 +171,107 @@
     return (attended_f + mixture).astype(jnp.bfloat16)
 
 
+def head_parallel_body(
+    queries,
+    new_kv,
+    cache_kv,
+    cache_spans,
+    recompute_rows,
+    held_states,
+    key_weight,
+    norm_gain,
+    routes,
+    route_weights,
+    expert_gate_up,
+    expert_down,
+):
+    seq_index = lax.axis_index("seq")
+    seq_count = lax.axis_size("seq")
+    req_index = lax.axis_index("req")
+    owner_count = lax.axis_size("req")
+    req_rows, tok_rows, model_width = queries.shape
+    cache_rows = cache_kv.shape[2]
+    held_rows = held_states.shape[1]
+    local_experts = expert_gate_up.shape[0]
+    groups = H // KVH
+    bf16 = jnp.bfloat16
+    f32 = jnp.float32
+    my_positions = lax.dynamic_slice_in_dim(recompute_rows, seq_index * held_rows, held_rows, 1)
+    projected = jnp.dot(
+        held_states.reshape(req_rows * held_rows, model_width),
+        key_weight,
+        preferred_element_type=f32,
+    )
+    rotated = rotate(projected.reshape(req_rows, held_rows, KVH, HD), my_positions).astype(bf16)
+    kv = jnp.concatenate([cache_kv, new_kv], axis=2)
+    kv = kv.reshape(2, req_rows, cache_rows + tok_rows, KVH, HD).transpose(3, 1, 2, 0, 4)
+    kv = kv.reshape(KVH, req_rows, cache_rows + tok_rows, 2 * HD)
+    kv = lax.all_to_all(kv, "seq", split_axis=0, concat_axis=0, tiled=True)
+    query_pack = queries.reshape(req_rows, tok_rows, KVH, groups * HD).transpose(2, 0, 1, 3)
+    query_pack = lax.all_to_all(query_pack, "seq", split_axis=0, concat_axis=0, tiled=True)
+    fresh = lax.all_to_all(
+        rotated.transpose(2, 0, 1, 3), "seq", split_axis=0, concat_axis=0, tiled=True
+    )
+    fresh = fresh.transpose(1, 0, 2, 3).reshape(req_rows, seq_count * held_rows, HD)
+    cache_total = seq_count * cache_rows
+    step_total = seq_count * tok_rows
+    cache_part = kv[:, :, :cache_rows].transpose(1, 0, 2, 3).reshape(req_rows, cache_total, 2 * HD)
+    step_part = kv[:, :, cache_rows:].transpose(1, 0, 2, 3).reshape(req_rows, step_total, 2 * HD)
+    positions = jnp.arange(cache_total)
+    hit_table = recompute_rows[:, None, :] == positions[None, :, None]
+    placed = jnp.einsum(
+        "rcm,rmk->rck", hit_table.astype(bf16), fresh, preferred_element_type=f32
+    ).astype(bf16)
+    cache_keys = jnp.where(jnp.any(hit_table, axis=2)[:, :, None], placed, cache_part[..., :HD])
+    keys = jnp.concatenate([cache_keys, step_part[..., :HD]], axis=1)
+    values = jnp.concatenate([cache_part[..., HD:], step_part[..., HD:]], axis=1)
+    heads = query_pack.reshape(seq_count, req_rows, tok_rows, groups, HD).transpose(1, 3, 0, 2, 4)
+    heads = heads.reshape(req_rows, groups, step_total, HD)
+    scores = jnp.einsum("rgqd,rnd->rgqn", heads, keys, preferred_element_type=f32) * HD ** (-0.5)
+    cache_allowed = (positions[None] >= cache_spans[:, 0:1]) & (positions[None] < cache_spans[:, 1:2])
+    step_allowed = jnp.arange(step_total)[None, :] <= jnp.arange(step_total)[:, None]
+    allowed = jnp.concatenate(
+        [
+            jnp.broadcast_to(cache_allowed[:, None, :], (req_rows, step_total, cache_total)),
+            jnp.broadcast_to(step_allowed[None], (req_rows, step_total, step_total)),
+        ],
+        axis=2,
+    )
+    scores = jnp.where(allowed[:, None], scores, NEG)
+    exps = jnp.exp(scores - jnp.max(scores, axis=-1, keepdims=True))
+    totals = jnp.sum(exps, axis=-1, keepdims=True)
+    mixed = jnp.einsum("rgqn,rnd->rgqd", exps.astype(bf16), values, preferred_element_type=f32)
+    mixed = (mixed / totals).astype(bf16)
+    mixed = mixed.reshape(req_rows, groups, seq_count, tok_rows, HD).transpose(2, 0, 3, 1, 4)
+    mixed = mixed.reshape(seq_count, req_rows, tok_rows, groups * HD)
+    mixed = lax.all_to_all(mixed, "seq", split_axis=0, concat_axis=0, tiled=True)
+    attended = mixed.transpose(1, 2, 0, 3).reshape(req_rows * tok_rows, model_width)
+    attended_f = attended.astype(f32)
+    mean_square = jnp.mean(attended_f * attended_f, axis=-1, keepdims=True)
+    normed = (attended_f * lax.rsqrt(mean_square + 1e-06) * norm_gain).astype(bf16)
+    tokens = lax.all_gather(normed, "req", axis=0, tiled=True)
+    all_routes = lax.all_gather(routes.reshape(req_rows * tok_rows, TOP), "req", axis=0, tiled=True)
+    all_weights = lax.all_gather(
+        route_weights.reshape(req_rows * tok_rows, TOP), "req", axis=0, tiled=True
+    )
+    mine = req_index * local_experts + jnp.arange(local_experts)
+    share = jnp.sum(
+        jnp.where(all_routes[:, :, None] == mine[None, None], all_weights[:, :, None], 0.0), axis=1
+    )
+    total = jnp.zeros(tokens.shape, f32)
+    for e in range(local_experts):
+        hidden = jnp.dot(tokens, expert_gate_up[e], preferred_element_type=f32)
+        active = (jax.nn.silu(hidden[:, :FF]) * hidden[:, FF:]).astype(bf16)
+        result = jnp.dot(active, expert_down[e], preferred_element_type=f32).astype(bf16)
+        total = total + result.astype(f32) * share[:, e : e + 1]
+    pieces = total.astype(bf16).reshape(owner_count, req_rows * tok_rows, model_width)
+    pieces = lax.all_to_all(pieces, "req", split_axis=0, concat_axis=0, tiled=True)
+    mixture = jnp.sum(pieces.astype(f32), axis=0)
+    return (attended_f + mixture).astype(bf16).reshape(req_rows, tok_rows, model_width)
+
+
 def solution(mesh):
+    body = head_parallel_body if mesh.shape["seq"] == KVH else body_wide
     in_specs = (
         P("req", "seq", None),
         P(None, "req", "seq", None),

time: 303 us -> 175 us (0.58)
  local copies, waits for them, and re-layouts: 102 us -> 18.3 us
  waiting for transfers between devices: 67.4 us -> 41.1 us
  blocking collectives: 67.7 us -> 46.3 us
  between operations: 13.9 us -> 0.49 us
  starting transfers between devices: 9.69 us -> 21.7 us
  matrix products: 26.3 us -> 34.2 us
    all_to_all x2 -> x0, blocking collectives: 56.9 us -> none  [the longest x1 50.3 us: body(): lax.all_to_all(outgoing, 'req', split_axis=0, concat_axis=0, tiled=True)]
    dynamic_update_slice x6 -> x0, local copies, waits for them, and re-layouts: 53.2 us -> none  [body(): lax.map(partial_attend, (all_queries, key_rows, value_rows, allowed))]
    all_gather x1 -> x3, blocking collectives: 10.8 us -> 46.3 us  [the longest x1 19.9 us: head_parallel_body(): tokens = lax.all_gather(normed, 'req', axis=0, tiled=True)]
    all_to_all x2 -> x5, waiting for transfers between devices: 57.1 us -> 41.1 us  [the longest x1 18.2 us: head_parallel_body(): lax.all_to_all(pieces, 'req', split_axis=0, concat_axis=0, tiled=True)]
    all_to_all x2 -> x5, starting transfers between devices: 9.69 us -> 21.7 us  [the longest x1 4.94 us: head_parallel_body(): kv = lax.all_to_all(kv, 'seq', split_axis=0, concat_axis=0, tiled=True)]
    mul x2 -> x0, local copies, waits for them, and re-layouts: 11.1 us -> none  [body(): spread_out * factors[..., None]]
    all_gather x1 -> x0, waiting for transfers between devices: 10.3 us -> none  [body(): all_queries = lax.all_gather(queries, 'seq', axis=1, tiled=True)]
    dot_general x10 -> x14, matrix products: 26.3 us -> 34.2 us  [the longest x5 14.9 us: head_parallel_body(): hidden = jnp.dot(tokens, expert_gate_up[e], preferred_element_type=f32)]
  transfers between devices with their start and end apart: 3 -> 5, of which waited for: 3 -> 4; matrix products, arithmetic and copies ran while one was open for 11% -> 4% of each run, Pallas kernels for 0% -> 0%
where the time goes in v1:
time: 175 us; the launch traced here: 173 us
  blocking collectives  46.3 us (26%)
  waiting for transfers between devices  41.1 us (23%)
  matrix products  34.2 us (20%)
  starting transfers between devices  21.7 us (12%)
  local copies, waits for them, and re-layouts  18.3 us (10%)
  other arithmetic  11.2 us (6%)
    all_gather x1, blocking collectives, head_parallel_body(): tokens = lax.all_gather(normed, 'req', axis=0, tiled=True)  19.9 us
    all_to_all x1, waiting for transfers between devices, head_parallel_body(): lax.all_to_all(pieces, 'req', split_axis=0, concat_axis=0, tiled=True)  18.2 us
    dot_general x5, matrix products, head_parallel_body(): hidden = jnp.dot(tokens, expert_gate_up[e], preferred_element_type=f32)  14.9 us
    all_gather x1, blocking collectives, head_parallel_body(): lax.all_gather(route_weights.reshape(req_rows * tok_rows, TOP), 'req', ax...  13.3 us
    all_gather x1, blocking collectives, head_parallel_body(): lax.all_gather(routes.reshape(req_rows * tok_rows, TOP), 'req', axis=0, t...  13.1 us
    all_to_all x1, waiting for transfers between devices, head_parallel_body(): kv = lax.all_to_all(kv, 'seq', split_axis=0, concat_axis=0, tiled=True)  12.1 us
    reduce_sum x1, other arithmetic, head_parallel_body(): totals = jnp.sum(exps, axis=-1, keepdims=True)  8.13 us
    dot_general x1, matrix products, head_parallel_body(): jnp.einsum('rgqn,rnd->rgqd', exps.astype(bf16), values, preferred_element...  7.03 us
  transfers between devices with their start and end apart: 5, of which 4 were waited for; matrix products, arithmetic and copies ran while one was open for 4% of the time, Pallas kernels for 0%

profile of v1, /device:TPU:2, one launch (start us, length us, event | category | flops | bytes accessed | tf_op | source)
XLA Modules:
  0.0 173.3 jit_solution(13547308417040345744)
XLA Ops:
  0.0 1.8 %copy.124 = bf16[1536,512]{0,1:T(8,128)(2,1)S(1)} copy(bf16[1536,512]{1,0:T(8,128)(2,1)} %param.18) | data formatting | bytes 3145728 | tf_op args[6]
  1.9 0.2 multiply_cosine_fusion
  2.1 0.9 fusion.78
  3.0 0.1 subtract_convert_fusion
  3.2 0.1 maximum_bitcast_fusion.4
  3.3 0.8 reshape.168
  4.1 4.3 %all-to-all-start = ((bf16[8,2,2048]{2,1,0:T(2,128)(2,1)}), bf16[8,2,2048]{2,1,0:T(2,128)(2,1)S(1)}, u32[]{:S(2)}, u32[]{:S(2)}) async-start(bf16[8,2,2048]{2,1,0:T(2,128)(2,1)} %reshape.168), calls=%async_computation | async-start | bytes 131072 | tf_op jit(solution)/shard_map/all_to_all | solution.py:212
  8.5 13.3 %all-gather.1 = f32[4,64,8]{1,2,0:T(8,128)S(1)} all-gather(f32[1,64,8]{1,2,0:T(8,128)S(1)} %reshape.158), channel_id=1, replica_groups=mesh['seq'=8,'req'=4] {'req'}, dimensions={0}, use_global_device_ids=true | all-gather | bytes 10240 | tf_op jit(solution)/shard_map/all_gather | solution.py:254
  22.0 13.1 %all-gather = s32[4,64,8]{1,2,0:T(8,128)S(1)} all-gather(s32[1,64,8]{1,2,0:T(8,128)S(1)} %reshape.156), channel_id=1, replica_groups=mesh['seq'=8,'req'=4] {'req'}, dimensions={0}, use_global_device_ids=true | all-gather | bytes 10240 | tf_op jit(solution)/shard_map/all_gather | solution.py:253
  35.2 0.2 reshape.146
  35.4 0.8 copy.158
  36.2 0.3 copy.129
  36.5 0.5 copy.128
  37.0 0.2 pad_maximum_fusion
  37.2 0.2 copy.130
  37.4 1.6 copy.131
  38.9 4.2 %all-to-all-start.2 = ((bf16[8,2,32,192]{3,2,1,0:T(8,128)(2,1)}), bf16[8,2,32,192]{3,2,1,0:T(8,128)(2,1)S(1)}, u32[]{:S(2)}, u32[]{:S(2)}) async-start(bf16[8,2,32,192]{3,2,1,0:T(8,128)(2,1)} %bitcast.120), calls=%async_computation.2 | async-start | bytes 524288 | tf_op jit(solution)/shard_map/all_to_all | solution.py:211
  43.3 5.3 %all-to-all-done.2 = bf16[8,2,32,192]{3,2,1,0:T(8,128)(2,1)S(1)} async-done(((bf16[8,2,32,192]{3,2,1,0:T(8,128)(2,1)}), bf16[8,2,32,192]{3,2,1,0:T(8,128)(2,1)S(1)}, u32[]{:S(2)}, u32[]{:S(2)}) %all-to-all-start.2) | async-done | bytes 196640 | tf_op jit(solution)/shard_map/all_to_all | solution.py:211
  48.6 4.9 %all-to-all-start.1 = ((bf16[8,2,288,128]{3,2,1,0:T(8,128)(2,1)}), bf16[8,2,288,128]{3,2,1,0:T(8,128)(2,1)S(1)}, u32[]{:S(2)}, u32[]{:S(2)}) async-start(bf16[8,2,288,128]{3,2,1,0:T(8,128)(2,1)} %copy.131), calls=%async_computation.1 | async-start | bytes 2359296 | tf_op jit(solution)/shard_map/all_to_all | solution.py:209
  53.6 0.2 slice_reduce_fusion.1
  53.7 0.6 fusion.7
  54.5 0.8 broadcast_in_dim.28
  55.4 0.4 pad_add_fusion
  55.8 0.1 reshape.169
  55.9 0.7 copy.126
  56.6 0.1 reshape.147
  56.8 12.1 %all-to-all-done.1 = bf16[8,2,288,128]{3,2,1,0:T(8,128)(2,1)S(1)} async-done(((bf16[8,2,288,128]{3,2,1,0:T(8,128)(2,1)}), bf16[8,2,288,128]{3,2,1,0:T(8,128)(2,1)S(1)}, u32[]{:S(2)}, u32[]{:S(2)}) %all-to-all-start.1) | async-done | bytes 1179680 | tf_op jit(solution)/shard_map/all_to_all | solution.py:209
  68.9 1.1 slice_bitcast_fusion
  70.0 2.6 %copy.132 = bf16[2,8,256,128]{2,1,3,0:T(8,128)(2,1)} copy(bf16[2,8,256,128]{3,2,0,1:T(8,128)(2,1)} %slice_bitcast_fusion) | data formatting | bytes 2097152 | tf_op jit(solution)/shard_map/transpose | solution.py:218
  72.6 2.3 %reshape.144 = bf16[2,2048,128]{1,2,0:T(8,128)(2,1)} reshape(bf16[2,8,256,128]{2,1,3,0:T(8,128)(2,1)} %copy.132) | data formatting | bytes 2097152 | tf_op jit(solution)/shard_map/reshape | solution.py:218
  75.0 0.1 fusion.89
  75.1 0.1 copy.155
  75.2 0.1 copy.156
  75.3 0.5 copy-done.6
  75.9 0.4 copy-done.2
  76.3 1.0 fusion.39
  77.3 6.4 %fusion.2 = (f32[2,3,256]{2,1,0:T(4,128)S(1)}, f32[2,2304,3,256]{3,1,2,0:T(8,128)}) fusion(pred[2,256,2304]{1,2,0:T(8,128)(4,1)S(1)} %pad_add_fusion, bf16[2,3,256,64]{3,2,1,0:T(8,128)(2,1)S(1)} %bitcast.129, bf16[2,256,64]{1,2,0:T(8,128)(2,1)S(1)} %copy.156, bf16[2,2048,64]{1,2,0:T(8,128)(2,1)S(1)} %fusion.39), kind=kOutput, calls=%fused_computation.4 | convolution fusion | flops 464779776 | bytes 16128000 | tf_op jit(solution)/shard_map/rgqd,rnd->rgqn/dot_general | solution.py:230
  83.7 8.1 %fusion = f32[2,3,256]{2,1,0:T(4,128)S(1)} fusion(f32[2,2304,3,256]{3,1,2,0:T(8,128)} %get-tuple-element.19, f32[2,3,256]{2,1,0:T(4,128)S(1)} %get-tuple-element.18, pred[2,256,2304]{1,2,0:T(8,128)(4,1)S(1)} %pad_add_fusion), kind=kLoop, calls=%fused_computation.2 | loop fusion | flops 14154240 | bytes 15347712 | tf_op jit(solution)/shard_map/reduce_sum | solution.py:242
  91.8 7.0 %fusion.54 = bf16[2,3,256,64]{2,3,1,0:T(8,128)(2,1)S(1)} fusion(f32[2,2304,3,256]{3,1,2,0:T(8,128)} %get-tuple-element.19, f32[2,3,256]{2,1,0:T(4,128)S(1)} %get-tuple-element.18, pred[2,256,2304]{1,2,0:T(8,128)(4,1)S(1)} %pad_add_fusion, bf16[2,256,64]{1,2,0:T(8,128)(2,1)S(1)} %copy.155, bf16[2,2048,64]{1,2,0:T(8,128)(2,1)S(1)} %slice-done, ...), kind=kOutput, calls=%fused_computation.63 | convolution fusion | flops 468516864 | bytes 16134144 | tf_op jit(solution)/shard_map/rgqn,rnd->rgqd/dot_general | solution.py:243
  98.8 0.2 copy.140
  99.1 0.3 copy.141
  99.4 1.0 reshape.150
  100.5 4.8 %all-to-all-start.3 = ((bf16[8,2,32,192]{3,2,1,0:T(8,128)(2,1)}), bf16[8,2,32,192]{3,2,1,0:T(8,128)(2,1)S(1)}, u32[]{:S(2)}, u32[]{:S(2)}) async-start(bf16[8,2,32,192]{3,2,1,0:T(8,128)(2,1)} %reshape.150), calls=%async_computation.3 | async-start | bytes 524288 | tf_op jit(solution)/shard_map/all_to_all | solution.py:247
  105.3 5.5 %all-to-all-done.3 = bf16[8,2,32,192]{3,2,1,0:T(8,128)(2,1)S(1)} async-done(((bf16[8,2,32,192]{3,2,1,0:T(8,128)(2,1)}), bf16[8,2,32,192]{3,2,1,0:T(8,128)(2,1)S(1)}, u32[]{:S(2)}, u32[]{:S(2)}) %all-to-all-start.3) | async-done | bytes 196640 | tf_op jit(solution)/shard_map/all_to_all | solution.py:247
  110.8 0.1 fusion.62
  111.1 0.3 copy.142
  111.4 0.2 reshape.155
  111.6 0.1 multiply_convert_fusion
  111.7 19.9 %all_gather.9 = bf16[256,1536]{1,0:T(8,128)(2,1)S(1)} all-gather(bf16[64,1536]{1,0:T(8,128)(2,1)S(1)} %multiply_convert_fusion), channel_id=1, replica_groups=mesh['seq'=8,'req'=4] {'req'}, dimensions={0}, use_global_device_ids=true | all-gather | bytes 983040 | tf_op jit(solution)/shard_map/all_gather | solution.py:252
  131.6 2.9 %fusion.8 = f32[256,1024]{1,0:T(8,128)S(1)} fusion(bf16[256,1536]{1,0:T(8,128)(2,1)S(1)} %all_gather.9, bf16[5,1536,1024]{2,1,0:T(8,128)(2,1)} %param.22), kind=kOutput, calls=%fused_computation.11 | convolution fusion | flops 805306368 | bytes 4980736 | tf_op jit(solution)/shard_map/dot_general | solution.py:263
  134.5 2.9 %fusion.10 = f32[256,1024]{1,0:T(8,128)S(1)} fusion(bf16[256,1536]{1,0:T(8,128)(2,1)S(1)} %all_gather.9, bf16[5,1536,1024]{2,1,0:T(8,128)(2,1)} %param.22), kind=kOutput, calls=%fused_computation.13 | convolution fusion | flops 805306368 | bytes 4980736 | tf_op jit(solution)/shard_map/dot_general | solution.py:263
  137.5 3.1 %fusion.12 = f32[256,1024]{1,0:T(8,128)S(1)} fusion(bf16[256,1536]{1,0:T(8,128)(2,1)S(1)} %all_gather.9, bf16[5,1536,1024]{2,1,0:T(8,128)(2,1)} %param.22), kind=kOutput, calls=%fused_computation.15 | convolution fusion | flops 805306368 | bytes 4980736 | tf_op jit(solution)/shard_map/dot_general | solution.py:263
  140.6 3.1 %fusion.14 = f32[256,1024]{1,0:T(8,128)S(1)} fusion(bf16[256,1536]{1,0:T(8,128)(2,1)S(1)} %all_gather.9, bf16[5,1536,1024]{2,1,0:T(8,128)(2,1)} %param.22), kind=kOutput, calls=%fused_computation.17 | convolution fusion | flops 805306368 | bytes 4980736 | tf_op jit(solution)/shard_map/dot_general | solution.py:263
  143.7 2.9 %fusion.16 = f32[256,1024]{1,0:T(8,128)S(1)} fusion(bf16[256,1536]{1,0:T(8,128)(2,1)S(1)} %all_gather.9, bf16[5,1536,1024]{2,1,0:T(8,128)(2,1)} %param.22), kind=kOutput, calls=%fused_computation.19 | convolution fusion | flops 805306368 | bytes 4980736 | tf_op jit(solution)/shard_map/dot_general | solution.py:263
  146.6 0.6 fusion.37
  147.2 0.6 fusion.35
  147.8 0.6 fusion.32
  148.5 0.6 fusion.29
  149.1 1.5 fusion.26
  150.6 3.5 %all-to-all-start.4 = ((bf16[4,64,1536]{2,1,0:T(8,128)(2,1)}), bf16[4,64,1536]{2,1,0:T(8,128)(2,1)S(1)}, u32[]{:S(2)}, u32[]{:S(2)}) async-start(bf16[4,64,1536]{2,1,0:T(8,128)(2,1)} %bitcast.41), calls=%async_computation.4 | async-start | bytes 1572864 | tf_op jit(solution)/shard_map/all_to_all | solution.py:268
  154.1 0.2 reshape.154
  154.3 18.2 %all-to-all-done.4 = bf16[4,64,1536]{2,1,0:T(8,128)(2,1)S(1)} async-done(((bf16[4,64,1536]{2,1,0:T(8,128)(2,1)}), bf16[4,64,1536]{2,1,0:T(8,128)(2,1)S(1)}, u32[]{:S(2)}, u32[]{:S(2)}) %all-to-all-start.4) | async-done | bytes 786464 | tf_op jit(solution)/shard_map/all_to_all | solution.py:268
  172.5 0.1 convert_reduce_fusion
  172.6 0.7 add_convert_fusion
  (53 shorter events, 1.0 us)
Async XLA Ops:
  0.0 2.1 %copy-start = (bf16[2,32,1536]{2,1,0:T(8,128)(2,1)S(1)}, bf16[2,32,1536]{2,1,0:T(8,128)(2,1)}, u32[]{:S(2)}) copy-start(bf16[2,32,1536]{2,1,0:T(8,128)(2,1)} %param.17) | copy-start | bytes 589828
  0.0 1.8 %copy-start.10 = (s32[2,256]{1,0:T(2,128)S(1)}, s32[2,256]{1,0:T(2,128)}, u32[]{:S(2)}) copy-start(s32[2,256]{1,0:T(2,128)} %param.16) | copy-start | bytes 6148
  2.1 6.3 %copy-start.8 = (s32[2,32,8]{1,2,0:T(8,128)S(1)}, s32[2,32,8]{1,2,0:T(8,128)}, u32[]{:S(2)}) copy-start(s32[2,32,8]{1,2,0:T(8,128)} %param.20) | copy-start | bytes 6148
  2.1 6.3 %copy-start.9 = (f32[2,32,8]{1,2,0:T(8,128)S(1)}, f32[2,32,8]{1,2,0:T(8,128)}, u32[]{:S(2)}) copy-start(f32[2,32,8]{1,2,0:T(8,128)} %param.21) | copy-start | bytes 6148
  2.1 33.1 %copy-start.4 = (bf16[2,32,1536]{2,1,0:T(8,128)(2,1)S(1)}, bf16[2,32,1536]{2,1,0:T(8,128)(2,1)}, u32[]{:S(2)}) copy-start(bf16[2,32,1536]{2,1,0:T(8,128)(2,1)} %param.12) | copy-start | bytes 589828
  3.0 33.2 %copy-start.5 = (bf16[2,2,32,512]{3,2,1,0:T(8,128)(2,1)S(1)}, bf16[2,2,32,512]{3,2,1,0:T(8,128)(2,1)}, u32[]{:S(2)}) copy-start(bf16[2,2,32,512]{3,2,1,0:T(8,128)(2,1)} %param.13) | copy-start | bytes 393220
  3.2 33.3 %copy-start.3 = (bf16[2,2,256,512]{3,2,1,0:T(8,128)(2,1)S(1)}, bf16[2,2,256,512]{3,2,1,0:T(8,128)(2,1)}, u32[]{:S(2)}) copy-start(bf16[2,2,256,512]{3,2,1,0:T(8,128)(2,1)} %param.14) | copy-start | bytes 3145732
  4.1 34.8 %all-to-all-start = ((bf16[8,2,2048]{2,1,0:T(2,128)(2,1)}), bf16[8,2,2048]{2,1,0:T(2,128)(2,1)S(1)}, u32[]{:S(2)}, u32[]{:S(2)}) async-start(bf16[8,2,2048]{2,1,0:T(2,128)(2,1)} %reshape.168), calls=%async_computation | async-start | bytes 131072 | tf_op jit(solution)/shard_map/all_to_all | solution.py:212
  38.9 14.6 %copy-start.11 = (s32[2,2]{1,0:T(2,128)S(1)}, s32[2,2]{1,0:T(2,128)}, u32[]{:S(2)}) copy-start(s32[2,2]{1,0:T(2,128)} %param.15) | copy-start | bytes 52
  38.9 9.7 %all-to-all-start.2 = ((bf16[8,2,32,192]{3,2,1,0:T(8,128)(2,1)}), bf16[8,2,32,192]{3,2,1,0:T(8,128)(2,1)S(1)}, u32[]{:S(2)}, u32[]{:S(2)}) async-start(bf16[8,2,32,192]{3,2,1,0:T(8,128)(2,1)} %bitcast.120), calls=%async_computation.2 | async-start | bytes 524288 | tf_op jit(solution)/shard_map/all_to_all | solution.py:211
  48.6 20.3 %all-to-all-start.1 = ((bf16[8,2,288,128]{3,2,1,0:T(8,128)(2,1)}), bf16[8,2,288,128]{3,2,1,0:T(8,128)(2,1)S(1)}, u32[]{:S(2)}, u32[]{:S(2)}) async-start(bf16[8,2,288,128]{3,2,1,0:T(8,128)(2,1)} %copy.131), calls=%async_computation.1 | async-start | bytes 2359296 | tf_op jit(solution)/shard_map/all_to_all | solution.py:209
  75.0 0.9 copy-start.6
  75.0 1.3 copy-start.2
  83.7 8.1 %slice-start = ((bf16[2,2048,128]{1,2,0:T(8,128)(2,1)}), bf16[2,2048,64]{1,2,0:T(8,128)(2,1)S(1)}, s32[]{:S(2)}) async-start(bf16[2,2048,128]{1,2,0:T(8,128)(2,1)} %reshape.144), calls=%async_computation.5 | async-start | bytes 1048576 | tf_op jit(solution)/shard_map/slice | solution.py:227
  100.5 10.3 %all-to-all-start.3 = ((bf16[8,2,32,192]{3,2,1,0:T(8,128)(2,1)}), bf16[8,2,32,192]{3,2,1,0:T(8,128)(2,1)S(1)}, u32[]{:S(2)}, u32[]{:S(2)}) async-start(bf16[8,2,32,192]{3,2,1,0:T(8,128)(2,1)} %reshape.150), calls=%async_computation.3 | async-start | bytes 524288 | tf_op jit(solution)/shard_map/all_to_all | solution.py:247
  105.3 6.3 %copy-start.7 = (f32[1536]{0:T(1024)S(1)}, f32[1536]{0:T(1024)}, u32[]{:S(2)}) copy-start(f32[1536]{0:T(1024)} %param.19) | copy-start | bytes 18436
  137.5 9.1 %slice-start.1 = ((s8[7864320]{0:T(1024)(128)(4,1)}), s8[4194304]{0:T(1024)(128)(4,1)S(1)}, s32[]{:S(2)}) async-start(s8[7864320]{0:T(1024)(128)(4,1)} %bitcast.136), calls=%async_computation.6 | async-start | bytes 8388608
  140.6 6.0 %slice-start.2 = ((s8[7864320]{0:T(1024)(128)(4,1)}), s8[3670016]{0:T(1024)(128)(4,1)S(1)}, s32[]{:S(2)}) async-start(s8[7864320]{0:T(1024)(128)(4,1)} %bitcast.136), calls=%async_computation.7 | async-start | bytes 7340032
  150.6 21.9 %all-to-all-start.4 = ((bf16[4,64,1536]{2,1,0:T(8,128)(2,1)}), bf16[4,64,1536]{2,1,0:T(8,128)(2,1)S(1)}, u32[]{:S(2)}, u32[]{:S(2)}) async-start(bf16[4,64,1536]{2,1,0:T(8,128)(2,1)} %bitcast.41), calls=%async_computation.4 | async-start | bytes 1572864 | tf_op jit(solution)/shard_map/all_to_all | solution.py:268
  154.1 19.2 %copy-start.1 = (bf16[2,32,1536]{2,1,0:T(8,128)(2,1)S(1)}, bf16[2,32,1536]{2,1,0:T(8,128)(2,1)}, u32[]{:S(2)}) copy-start(bf16[2,32,1536]{2,1,0:T(8,128)(2,1)} %param.17) | copy-start | bytes 589828

commit v2 on v0

--- a/solution.py
+++ b/solution.py
@@ -1,6 +1,8 @@
 import jax
 import jax.numpy as jnp
 from jax import lax
+from jax.experimental import pallas as pl
+from jax.experimental.pallas import tpu as pltpu
 from jax.sharding import PartitionSpec as P
 
 H = 24
@@ -58,7 +60,7 @@
     return (mixed_rows.reshape(query_count, model_width), log_rows)
 
 
-def body(
+def body_wide(
     queries,
     new_kv,
     cache_kv,
@@ -171,7 +173,386 @@
     return (attended_f + mixture).astype(jnp.bfloat16)
 
 
+def layer_kernel(
+    spans_ref,
+    rec_ref,
+    cos_ref,
+    sin_ref,
+    q_ref,
+    new_ref,
+    cache_ref,
+    held_ref,
+    kw_ref,
+    gain_ref,
+    routes_ref,
+    rw_ref,
+    gu_hbm,
+    dn_hbm,
+    out_ref,
+    gu_v,
+    dn_v,
+    kvsend,
+    stsend,
+    qsend,
+    fsend,
+    osend,
+    crecv,
+    srecv,
+    qrecv,
+    frecv,
+    orecv,
+    kbuf,
+    vbuf,
+    att,
+    trecv,
+    wrecv,
+    total,
+    psend,
+    precv,
+    load_sem,
+    s_sem,
+    r_sem,
+    zs_sem,
+    zr_sem,
+):
+    bf16 = jnp.bfloat16
+    f32 = jnp.float32
+    me = lax.axis_index("seq")
+    S = lax.axis_size("seq")
+    mz = lax.axis_index("req")
+    N = lax.axis_size("req")
+    groups = H // KVH
+    tok = q_ref.shape[1]
+    crows = cache_ref.shape[2]
+    held = frecv.shape[0] // S
+    width = q_ref.shape[2]
+    local_experts = gu_v.shape[0]
+    ctotal = S * crows
+    stotal = S * tok
+
+    barrier = pltpu.get_barrier_semaphore()
+    for k in range(1, S):
+        pl.semaphore_signal(barrier, inc=1, device_id={"seq": lax.rem(me + k, S)})
+    for k in range(1, N):
+        pl.semaphore_signal(barrier, inc=1, device_id={"req": lax.rem(mz + k, N)})
+
+    def lanes(rows):
+        return lax.broadcasted_iota(jnp.int32, (rows, 2 * HD), 1)
+
+    def join(low, low_roll, high, high_roll, scale=None):
+        a, b = low.astype(f32), high.astype(f32)
+        a = pltpu.roll(a, HD, 1) if low_roll else a
+        b = pltpu.roll(b, HD, 1) if high_roll else b
+        c = jnp.where(lanes(a.shape[0]) < HD, a, b)
+        return (c if scale is None else c * scale).astype(bf16)
+
+    for h in range(KVH):
+        cols = slice((h // 2) * 2 * HD, (h // 2 + 1) * 2 * HD)
+        odd = h % 2 == 1
+        for g in range(groups):
+            c = h * groups + g
+            qc = slice((c // 2) * 2 * HD, (c // 2 + 1) * 2 * HD)
+            qsend[h, g] = join(q_ref[0, :, qc], c % 2 == 1, q_ref[1, :, qc], c % 2 == 0, HD**-0.5)
+        for src, dst in ((cache_ref, kvsend), (new_ref, stsend)):
+            dst[h, 0] = join(src[0, 0, :, cols], odd, src[1, 0, :, cols], not odd)
+            dst[h, 1] = join(src[1, 1, :, cols], odd, src[0, 1, :, cols], not odd)
+
+    def row_at(i, n):
+        return pl.ds(pl.multiple_of(i * n, n), n)
+
+    def exchange(kind, k, slot):
+        peer = lax.rem(me + k, S)
+        src, dst = (
+            (qsend.at[peer], qrecv.at[:, row_at(slot, tok), :]),
+            (stsend.at[peer], srecv.at[:, row_at(slot, tok), :]),
+            (kvsend.at[peer, 0], crecv.at[0, row_at(slot, crows), :]),
+            (kvsend.at[peer, 1], crecv.at[1, row_at(slot, crows), :]),
+            (fsend.at[peer], frecv.at[row_at(slot, held), :]),
+            (osend.at[:, row_at(peer, tok), :], orecv.at[slot]),
+        )[kind]
+        return pltpu.make_async_remote_copy(
+            src_ref=src,
+            dst_ref=dst,
+            send_sem=s_sem.at[kind, k],
+            recv_sem=r_sem.at[kind, k],
+            device_id={"seq": peer},
+        )
+
+    def arrive(kind):
+        for k in range(1, S):
+            exchange(kind, k, lax.rem(me + S - k, S)).wait_recv()
+
+    pl.semaphore_wait(barrier, S - 1 + N - 1)
+    for k in range(1, S):
+        for kind in (0, 1, 2):
+            exchange(kind, k, me).start()
+
+    loads = []
+    for e in range(local_experts):
+        loads.append(pltpu.make_async_copy(gu_hbm.at[e], gu_v.at[e], load_sem.at[0, e]))
+        loads.append(pltpu.make_async_copy(dn_hbm.at[e], dn_v.at[e], load_sem.at[1, e]))
+
+    fresh = jnp.dot(held_ref[...], kw_ref[...], preferred_element_type=f32)
+    low_part = lax.broadcasted_iota(jnp.int32, fresh.shape, 1) % HD < HD // 2
+    partner = jnp.where(
+        low_part,
+        pltpu.roll(fresh, fresh.shape[1] - HD // 2, 1),
+        pltpu.roll(fresh, HD // 2, 1),
+    )
+    fresh = fresh * jnp.tile(cos_ref[...], (1, KVH // 2)) + partner * jnp.tile(
+        sin_ref[...], (1, KVH // 2)
+    )
+    for h in range(KVH):
+        cols = slice((h // 2) * 2 * HD, (h // 2 + 1) * 2 * HD)
+        odd = h % 2 == 1
+        fsend[h] = join(fresh[:held, cols], odd, fresh[held:, cols], not odd)
+    for k in range(1, S):
+        exchange(4, k, me).start()
+    for k in range(1, S):
+        exchange(3, k, me).start()
+    for load in loads:
+        load.start()
+
+    qrecv[:, row_at(me, tok), :] = qsend[me]
+    srecv[:, row_at(me, tok), :] = stsend[me]
+    crecv[:, row_at(me, crows), :] = kvsend[me]
+    frecv[row_at(me, held), :] = fsend[me]
+
+    expert_lane = lax.broadcasted_iota(jnp.int32, (2 * tok, 128), 1)
+    dense = jnp.zeros((2 * tok, 128), f32)
+    for k in range(TOP):
+        dense = dense + jnp.where(routes_ref[:, k : k + 1] == expert_lane, rw_ref[:, k : k + 1], 0.0)
+    wrecv[mz] = dense
+
+    def across(kind, k, slot):
+        peer = lax.rem(mz + k, N)
+        src, dst = (
+            (wrecv.at[mz], wrecv.at[slot]),
+            (trecv.at[mz], trecv.at[slot]),
+            (psend.at[peer], precv.at[slot]),
+        )[kind]
+        return pltpu.make_async_remote_copy(
+            src_ref=src,
+            dst_ref=dst,
+            send_sem=zs_sem.at[kind, k],
+            recv_sem=zr_sem.at[kind, k],
+            device_id={"req": peer},
+        )
+
+    def across_arrive(kind):
+        for k in range(1, N):
+            across(kind, k, lax.rem(mz + N - k, N)).wait_recv()
+
+    for k in range(1, N):
+        across(0, k, mz).start()
+
+    for kind in (0, 1, 2, 4):
+        arrive(kind)
+    for r in range(2):
+        if r == 1:
+            arrive(3)
+        key_half = (lanes(crows) < HD) if r == 0 else (lanes(crows) >= HD)
+        ones = jnp.ones((S * held, 2 * HD), bf16)
+        spread = jnp.concatenate([frecv[...], ones], axis=1)
+        wanted = rec_ref[r : r + 1, :]
+
+        def place(i, carry):
+            rows = row_at(i, crows)
+            kv = crecv[r, rows, :].astype(f32)
+            where_to = lax.broadcasted_iota(jnp.int32, (crows, S * held), 0) + i * crows
+            hit = jnp.where(where_to == wanted, 1.0, 0.0).astype(bf16)
+            both = jnp.dot(hit, spread, preferred_element_type=f32)
+            keys = jnp.where(both[:, 2 * HD :] > 0.5, both[:, : 2 * HD], kv)
+            kbuf[rows, :] = jnp.where(key_half, keys, 0.0).astype(bf16)
+            vbuf[rows, :] = jnp.where(key_half, 1.0, kv).astype(bf16)
+            return carry
+
+        lax.fori_loop(0, S, place, 0)
+        step = srecv[r].astype(f32)
+        step_half = (lanes(stotal) < HD) if r == 0 else (lanes(stotal) >= HD)
+        kbuf[ctotal:, :] = jnp.where(step_half, step, 0.0).astype(bf16)
+        vbuf[ctotal:, :] = jnp.where(step_half, 1.0, step).astype(bf16)
+        position = lax.broadcasted_iota(jnp.int32, (1, ctotal), 1)
+        open_row = (position >= spans_ref[r, 0]) & (position < spans_ref[r, 1])
+        bias = jnp.where(open_row, 0.0, NEG)
+        causal = lax.broadcasted_iota(jnp.int32, (stotal, stotal), 1) <= lax.broadcasted_iota(
+            jnp.int32, (stotal, stotal), 0
+        )
+        contract = (((1,), (1,)), ((), ()))
+
+        def attend(g, carry):
+            query = qrecv[g]
+            old = lax.dot_general(
+                query, kbuf[:ctotal, :], contract, preferred_element_type=f32
+            ) + bias
+            new = lax.dot_general(query, kbuf[ctotal:, :], contract, preferred_element_type=f32)
+            new = jnp.where(causal, new, NEG)
+            highest = jnp.maximum(
+                jnp.max(old, axis=-1, keepdims=True), jnp.max(new, axis=-1, keepdims=True)
+            )
+            mixed = jnp.dot(
+                jnp.exp(old - highest).astype(bf16), vbuf[:ctotal, :], preferred_element_type=f32
+            ) + jnp.dot(
+                jnp.exp(new - highest).astype(bf16), vbuf[ctotal:, :], preferred_element_type=f32
+            )
+            mixed = mixed / pltpu.roll(mixed, HD, 1)
+            if r == 0:
+                osend[g] = mixed.astype(bf16)
+            else:
+                osend[g] = jnp.where(
+                    lanes(stotal) < HD, mixed, osend[g].astype(f32)
+                ).astype(bf16)
+            return carry
+
+        lax.fori_loop(0, groups, attend, 0)
+
+    for k in range(1, S):
+        exchange(5, k, me).start()
+    orecv[me] = osend[:, row_at(me, tok), :]
+    arrive(5)
+    for pair in range(H // 2):
+        first, second = 2 * pair, 2 * pair + 1
+        one = orecv[first // groups, first % groups]
+        two = orecv[second // groups, second % groups]
+        cols = slice(pair * 2 * HD, (pair + 1) * 2 * HD)
+        att[:tok, cols] = join(one, True, two, False)
+        att[tok:, cols] = join(one, False, two, True)
+    attended = att[...].astype(f32)
+    mean_square = jnp.mean(attended * attended, axis=-1, keepdims=True)
+    trecv[mz] = (attended * lax.rsqrt(mean_square + 1e-06) * gain_ref[...]).astype(bf16)
+    for k in range(1, N):
+        across(1, k, mz).start()
+    across_arrive(0)
+    for load in loads:
+        load.wait()
+    across_arrive(1)
+
+    tokens_total = N * 2 * tok
+    total[...] = jnp.zeros_like(total)
+
+    def expert(e, carry):
+        tokens = trecv[...].reshape(tokens_total, width)
+        hidden = jnp.dot(tokens, gu_v[e], preferred_element_type=f32)
+        gate, up = hidden[:, :FF], hidden[:, FF:]
+        active = (gate / (1.0 + jnp.exp(-gate)) * up).astype(bf16)
+        result = jnp.dot(active, dn_v[e], preferred_element_type=f32).astype(bf16)
+        weights = wrecv[...].reshape(tokens_total, 128)
+        lane = lax.broadcasted_iota(jnp.int32, weights.shape, 1)
+        share = jnp.sum(
+            jnp.where(lane == mz * local_experts + e, weights, 0.0), axis=1, keepdims=True
+        )
+        total[...] += result.astype(f32) * share
+        return carry
+
+    lax.fori_loop(0, local_experts, expert, 0)
+    psend[...] = total[...].astype(bf16).reshape(psend.shape)
+    for k in range(1, N):
+        across(2, k, mz).start()
+    mixture = att[...].astype(f32) + psend[mz].astype(f32)
+    across_arrive(2)
+    for k in range(1, N):
+        mixture = mixture + precv[lax.rem(mz + N - k, N)].astype(f32)
+    out_ref[...] = mixture.astype(bf16)
+    for kind in range(6):
+        for k in range(1, S):
+            exchange(kind, k, me).wait_send()
+    for kind in range(3):
+        for k in range(1, N):
+            across(kind, k, mz).wait_send()
+
+
+def head_parallel_body(
+    queries,
+    new_kv,
+    cache_kv,
+    cache_spans,
+    recompute_rows,
+    held_states,
+    key_weight,
+    norm_gain,
+    routes,
+    route_weights,
+    expert_gate_up,
+    expert_down,
+):
+    seq_index = lax.axis_index("seq")
+    S = lax.axis_size("seq")
+    N = lax.axis_size("req")
+    req_rows, tok, width = queries.shape
+    crows = cache_kv.shape[2]
+    held = held_states.shape[1]
+    local_experts = expert_gate_up.shape[0]
+    groups = H // KVH
+    bf16, f32 = jnp.bfloat16, jnp.float32
+    positions = lax.dynamic_slice_in_dim(recompute_rows, seq_index * held, held, 1)
+    half = HD // 2
+    inverse = THETA ** (-(jnp.arange(half).astype(f32) * (2.0 / HD)))
+    angles = positions.reshape(req_rows * held, 1).astype(f32) * inverse
+    cosine, sine = jnp.cos(angles), jnp.sin(angles)
+    cos_table = jnp.concatenate([cosine] * 4, axis=1)
+    sin_table = jnp.concatenate([-sine, sine, -sine, sine], axis=1)
+    vmem = pl.BlockSpec(memory_space=pltpu.VMEM)
+    smem = pl.BlockSpec(memory_space=pltpu.SMEM)
+    hbm = pl.BlockSpec(memory_space=pl.ANY)
+    lane = 2 * HD
+    rows = req_rows * tok
+    out = pl.pallas_call(
+        layer_kernel,
+        out_shape=jax.ShapeDtypeStruct((rows, width), bf16),
+        in_specs=[smem] + [vmem] * 11 + [hbm, hbm],
+        out_specs=vmem,
+        scratch_shapes=[
+            pltpu.VMEM(expert_gate_up.shape, bf16),
+            pltpu.VMEM(expert_down.shape, bf16),
+            pltpu.VMEM((S, 2, crows, lane), bf16),
+            pltpu.VMEM((S, 2, tok, lane), bf16),
+            pltpu.VMEM((S, groups, tok, lane), bf16),
+            pltpu.VMEM((S, held, lane), bf16),
+            pltpu.VMEM((groups, S * tok, lane), bf16),
+            pltpu.VMEM((2, S * crows, lane), bf16),
+            pltpu.VMEM((2, S * tok, lane), bf16),
+            pltpu.VMEM((groups, S * tok, lane), bf16),
+            pltpu.VMEM((S * held, lane), bf16),
+            pltpu.VMEM((S, groups, tok, lane), bf16),
+            pltpu.VMEM((S * (crows + tok), lane), bf16),
+            pltpu.VMEM((S * (crows + tok), lane), bf16),
+            pltpu.VMEM((rows, width), bf16),
+            pltpu.VMEM((N, rows, width), bf16),
+            pltpu.VMEM((N, rows, 128), f32),
+            pltpu.VMEM((N * rows, width), f32),
+            pltpu.VMEM((N, rows, width), bf16),
+            pltpu.VMEM((N, rows, width), bf16),
+            pltpu.SemaphoreType.DMA((2, local_experts)),
+            pltpu.SemaphoreType.DMA((6, S)),
+            pltpu.SemaphoreType.DMA((6, S)),
+            pltpu.SemaphoreType.DMA((3, N)),
+            pltpu.SemaphoreType.DMA((3, N)),
+        ],
+        compiler_params=pltpu.CompilerParams(
+            collective_id=0, has_side_effects=True, vmem_limit_bytes=60 << 20
+        ),
+        name="layer",
+    )(
+        cache_spans,
+        recompute_rows,
+        cos_table,
+        sin_table,
+        queries,
+        new_kv,
+        cache_kv,
+        held_states.reshape(req_rows * held, width),
+        key_weight,
+        norm_gain.reshape(1, width),
+        routes.reshape(rows, TOP),
+        route_weights.reshape(rows, TOP),
+        expert_gate_up,
+        expert_down,
+    )
+    return out.reshape(req_rows, tok, width)
+
+
 def solution(mesh):
+    body = head_parallel_body if mesh.shape["seq"] == KVH else body_wide
     in_specs = (
         P("req", "seq", None),
         P(None, "req", "seq", None),

time: 303 us -> 86 us (0.28)
  the two profiles are of different devices: /device:TPU:2 before, /device:TPU:26 now
where the time goes in v2:
time: 86 us; the launch traced here: 85.7 us
  Pallas kernels  78.2 us (91%)
  local copies, waits for them, and re-layouts  5.76 us (7%)
  other arithmetic  1.69 us (2%)
    pallas_call x1, Pallas kernels, head_parallel_body(): pl.pallas_call(layer_kernel, out_shape=jax.ShapeDtypeStruct((rows, width)...  78.2 us
    unnamed x3, local copies, waits for them, and re-layouts  4.37 us

profile of v2, /device:TPU:26, one launch (start us, length us, event | category | flops | bytes accessed | tf_op | source)
XLA Modules:
  0.0 85.7 jit_solution(15537740633784589160)
XLA Ops:
  0.0 0.8 dynamic-slice_convert_fusion
  0.8 0.1 convert_element_type.19
  0.8 1.3 %reshape.32.gain_ref = f32[1,1536]{1,0:T(1,128)} reshape(f32[1536]{0:T(1024)} %param.19) | data formatting | bytes 12288 | tf_op jit(solution)/shard_map/reshape | solution.py:545
  2.1 1.4 %copy.13 = s32[2,32,8]{2,1,0:T(8,128)} copy(s32[2,32,8]{1,2,0:T(8,128)} %param.20) | data formatting | bytes 4096 | tf_op args[8]
  3.5 1.4 %copy.14 = f32[2,32,8]{2,1,0:T(8,128)} copy(f32[2,32,8]{1,2,0:T(8,128)} %param.21) | data formatting | bytes 4096 | tf_op args[9]
  4.9 0.2 fusion
  5.1 0.7 pad_maximum_fusion
  5.8 78.2 %layer.1 = bf16[64,1536]{1,0:T(8,128)(2,1)} custom-call(s32[2,2]{1,0:T(2,128)} %spans_ref.1, s32[2,256]{1,0:T(2,128)} %rec_ref.1, f32[64,128]{1,0:T(8,128)} %get-tuple-element.8.cos_ref, f32[64,128]{1,0:T(8,128)} %get-tuple-element.9.sin_ref, bf16[2,32,1536]{2,1,0:T(8,128)(2,1)} %q_ref.1, bf16[2,2,32,512]{3,2,1,0:T(8,128)(2,1)} %new_ref.1, ...), custom_call_target="tpu_custom_call" | custom-call | tf_op jit(solution)/shard_map/layer/pallas_call | solution.py:499
  84.1 1.6 %copy.16 = bf16[2,32,1536]{2,1,0:T(8,128)(2,1)} copy(bf16[2,32,1536]{2,1,0:T(8,128)(2,1)} %bitcast.4) | data formatting | bytes 393216
  (1 shorter events, 0.0 us)

commit v3 on v2

--- a/solution.py
+++ b/solution.py
@@ -214,6 +214,8 @@
     r_sem,
     zs_sem,
     zr_sem,
+    ts_sem,
+    tr_sem,
 ):
     bf16 = jnp.bfloat16
     f32 = jnp.float32
@@ -318,33 +320,60 @@
     crecv[:, row_at(me, crows), :] = kvsend[me]
     frecv[row_at(me, held), :] = fsend[me]
 
-    expert_lane = lax.broadcasted_iota(jnp.int32, (2 * tok, 128), 1)
-    dense = jnp.zeros((2 * tok, 128), f32)
-    for k in range(TOP):
-        dense = dense + jnp.where(routes_ref[:, k : k + 1] == expert_lane, rw_ref[:, k : k + 1], 0.0)
-    wrecv[mz] = dense
-
-    def across(kind, k, slot):
+    expert_row = lax.broadcasted_iota(jnp.int32, (128, tok), 0)
+    for r in range(2):
+        dense = jnp.zeros((128, tok), f32)
+        for k in range(TOP):
+            hit = routes_ref[r, k : k + 1, :] == expert_row
+            dense = dense + jnp.where(hit, rw_ref[r, k : k + 1, :], 0.0)
+        wrecv[mz, r * tok : (r + 1) * tok, :] = dense.T
+
+    def share_copy(k, slot):
+        return pltpu.make_async_remote_copy(
+            src_ref=wrecv.at[mz],
+            dst_ref=wrecv.at[slot],
+            send_sem=zs_sem.at[0, k],
+            recv_sem=zr_sem.at[0, k],
+            device_id={"req": lax.rem(mz + k, N)},
+        )
+
+    def back_copy(r, k, slot):
         peer = lax.rem(mz + k, N)
-        src, dst = (
-            (wrecv.at[mz], wrecv.at[slot]),
-            (trecv.at[mz], trecv.at[slot]),
-            (psend.at[peer], precv.at[slot]),
-        )[kind]
         return pltpu.make_async_remote_copy(
-            src_ref=src,
-            dst_ref=dst,
-            send_sem=zs_sem.at[kind, k],
-            recv_sem=zr_sem.at[kind, k],
+            src_ref=psend.at[r, peer],
+            dst_ref=precv.at[r, slot],
+            send_sem=zs_sem.at[1 + r, k],
+            recv_sem=zr_sem.at[1 + r, k],
             device_id={"req": peer},
         )
 
-    def across_arrive(kind):
-        for k in range(1, N):
-            across(kind, k, lax.rem(mz + N - k, N)).wait_recv()
+    def token_copy(r, origin, way):
+        return pltpu.make_async_remote_copy(
+            src_ref=trecv.at[r, origin],
+            dst_ref=trecv.at[r, origin],
+            send_sem=ts_sem.at[way, r, origin],
+            recv_sem=tr_sem.at[r, origin],
+            device_id={"req": mz + 1 if way == 0 else mz - 1},
+        )
+
+    def send_tokens(r, origin, way):
+        @pl.when(mz < N - 1 if way == 0 else mz > 0)
+        def _():
+            token_copy(r, origin, way).start()
+
+    def relay(d, r):
+        @pl.when(mz - d >= 0)
+        def _():
+            token_copy(r, mz - d, 0).wait_recv()
+            send_tokens(r, mz - d, 0)
+
+        @pl.when(mz + d < N)
+        def _():
+            token_copy(r, mz + d, 1).wait_recv()
+            send_tokens(r, mz + d, 1)
 
     for k in range(1, N):
-        across(0, k, mz).start()
+        share_copy(k, mz).start()
 
     for kind in (0, 1, 2, 4):
         arrive(kind)
@@ -419,46 +448,66 @@
         att[tok:, cols] = join(one, False, two, True)
     attended = att[...].astype(f32)
     mean_square = jnp.mean(attended * attended, axis=-1, keepdims=True)
-    trecv[mz] = (attended * lax.rsqrt(mean_square + 1e-06) * gain_ref[...]).astype(bf16)
+    normed = (attended * lax.rsqrt(mean_square + 1e-06) * gain_ref[...].reshape(1, width)).astype(bf16)
+    for r in range(2):
+        trecv[r, mz] = normed[r * tok : (r + 1) * tok]
+        for way in range(2):
+            send_tokens(r, mz, way)
     for k in range(1, N):
-        across(1, k, mz).start()
-    across_arrive(0)
+        share_copy(k, lax.rem(mz + N - k, N)).wait_recv()
     for load in loads:
         load.wait()
-    across_arrive(1)
-
-    tokens_total = N * 2 * tok
-    total[...] = jnp.zeros_like(total)
-
-    def expert(e, carry):
-        tokens = trecv[...].reshape(tokens_total, width)
-        hidden = jnp.dot(tokens, gu_v[e], preferred_element_type=f32)
-        gate, up = hidden[:, :FF], hidden[:, FF:]
-        active = (gate / (1.0 + jnp.exp(-gate)) * up).astype(bf16)
-        result = jnp.dot(active, dn_v[e], preferred_element_type=f32).astype(bf16)
-        weights = wrecv[...].reshape(tokens_total, 128)
-        lane = lax.broadcasted_iota(jnp.int32, weights.shape, 1)
-        share = jnp.sum(
-            jnp.where(lane == mz * local_experts + e, weights, 0.0), axis=1, keepdims=True
-        )
-        total[...] += result.astype(f32) * share
-        return carry
-
-    lax.fori_loop(0, local_experts, expert, 0)
-    psend[...] = total[...].astype(bf16).reshape(psend.shape)
-    for k in range(1, N):
-        across(2, k, mz).start()
-    mixture = att[...].astype(f32) + psend[mz].astype(f32)
-    across_arrive(2)
-    for k in range(1, N):
-        mixture = mixture + precv[lax.rem(mz + N - k, N)].astype(f32)
-    out_ref[...] = mixture.astype(bf16)
+    for d in range(1, N - 1):
+        for r in range(2):
+            relay(d, r)
+    rows_total = N * tok
+    for r in range(2):
+        relay(N - 1, r)
+        total[...] = jnp.zeros_like(total)
+
+        def expert(e, carry):
+            tokens = trecv[r].reshape(rows_total, width)
+            hidden = jnp.dot(tokens, gu_v[e], preferred_element_type=f32)
+            gate, up = hidden[:, :FF], hidden[:, FF:]
+            active = (gate / (1.0 + jnp.exp(-gate)) * up).astype(bf16)
+            result = jnp.dot(active, dn_v[e], preferred_element_type=f32).astype(bf16)
+            weights = wrecv[:, r * tok : (r + 1) * tok, :].reshape(rows_total, 128)
+            lane = lax.broadcasted_iota(jnp.int32, weights.shape, 1)
+            share = jnp.sum(
+                jnp.where(lane == mz * local_experts + e, weights, 0.0), axis=1, keepdims=True
+            )
+            total[...] += result.astype(f32) * share
+            return carry
+
+        lax.fori_loop(0, local_experts, expert, 0)
+        psend[r] = total[...].astype(bf16).reshape(N, tok, width)
+        for k in range(1, N):
+            back_copy(r, k, mz).start()
+    for r in range(2):
+        rows = slice(r * tok, (r + 1) * tok)
+        mixture = att[rows, :].astype(f32) + psend[r, mz].astype(f32)
+        for k in range(1, N):
+            back_copy(r, k, lax.rem(mz + N - k, N)).wait_recv()
+        for k in range(1, N):
+            mixture = mixture + precv[r, lax.rem(mz + N - k, N)].astype(f32)
+        out_ref[rows, :] = mixture.astype(bf16)
     for kind in range(6):
         for k in range(1, S):
             exchange(kind, k, me).wait_send()
-    for kind in range(3):
-        for k in range(1, N):
-            across(kind, k, mz).wait_send()
+    for k in range(1, N):
+        share_copy(k, mz).wait_send()
+        for r in range(2):
+            back_copy(r, k, mz).wait_send()
+    for r in range(2):
+        for origin in range(N):
+
+            @pl.when((origin <= mz) & (mz < N - 1))
+            def _():
+                token_copy(r, origin, 0).wait_send()
+
+            @pl.when((origin >= mz) & (mz > 0))
+            def _():
+                token_copy(r, origin, 1).wait_send()
 
 
 def head_parallel_body(
@@ -517,16 +566,18 @@
             pltpu.VMEM((S * (crows + tok), lane), bf16),
             pltpu.VMEM((S * (crows + tok), lane), bf16),
             pltpu.VMEM((rows, width), bf16),
-            pltpu.VMEM((N, rows, width), bf16),
+            pltpu.VMEM((2, N, tok, width), bf16),
             pltpu.VMEM((N, rows, 128), f32),
-            pltpu.VMEM((N * rows, width), f32),
-            pltpu.VMEM((N, rows, width), bf16),
-            pltpu.VMEM((N, rows, width), bf16),
+            pltpu.VMEM((N * tok, width), f32),
+            pltpu.VMEM((2, N, tok, width), bf16),
+            pltpu.VMEM((2, N, tok, width), bf16),
             pltpu.SemaphoreType.DMA((2, local_experts)),
             pltpu.SemaphoreType.DMA((6, S)),
             pltpu.SemaphoreType.DMA((6, S)),
             pltpu.SemaphoreType.DMA((3, N)),
             pltpu.SemaphoreType.DMA((3, N)),
+            pltpu.SemaphoreType.DMA((2, 2, N)),
+            pltpu.SemaphoreType.DMA((2, N)),
         ],
         compiler_params=pltpu.CompilerParams(
             collective_id=0, has_side_effects=True, vmem_limit_bytes=60 << 20
@@ -542,9 +593,9 @@
         cache_kv,
         held_states.reshape(req_rows * held, width),
         key_weight,
-        norm_gain.reshape(1, width),
-        routes.reshape(rows, TOP),
-        route_weights.reshape(rows, TOP),
+        norm_gain,
+        jnp.transpose(routes, (0, 2, 1)),
+        jnp.transpose(route_weights, (0, 2, 1)),
         expert_gate_up,
         expert_down,
     )

time: 86 us -> 72.9 us (0.85)
  the two profiles are of different devices: /device:TPU:26 before, /device:TPU:2 now
where the time goes in v3:
time: 72.9 us; the launch traced here: 71.6 us
  Pallas kernels  68.2 us (94%)
  other arithmetic  1.7 us (2%)
  local copies, waits for them, and re-layouts  1.7 us (2%)
    pallas_call x1, Pallas kernels, head_parallel_body(): pl.pallas_call(layer_kernel, out_shape=jax.ShapeDtypeStruct((rows, width)...  68.2 us
    unnamed x1, local copies, waits for them, and re-layouts  1.62 us

profile of v3, /device:TPU:2, one launch (start us, length us, event | category | flops | bytes accessed | tf_op | source)
XLA Modules:
  0.0 71.6 jit_solution(14292444874766794913)
XLA Ops:
  0.0 0.8 %dynamic-slice_convert_fusion = f32[2,32]{1,0:T(2,128)S(1)} fusion(s32[2,256]{1,0:T(2,128)} %rec_ref.1, s32[]{:T(128)S(6)} %select_n.3), kind=kLoop, calls=%fused_computation.5 | loop fusion | flops 64 | bytes 516 | tf_op jit(solution)/shard_map/convert_element_type | solution.py:539
  0.8 0.1 convert_element_type.19
  0.8 0.2 fusion
  1.0 0.7 %pad_maximum_fusion = (f32[64,128]{1,0:T(8,128)}, f32[64,128]{1,0:T(8,128)}) fusion(f32[64,32]{1,0:T(8,128)S(1)} %get-tuple-element.7, f32[64,32]{1,0:T(8,128)S(1)} %get-tuple-element.6, f32[64,32]{1,0:T(8,128)S(1)} %get-tuple-element.5), kind=kLoop, calls=%fused_computation.2 | loop fusion | flops 49152 | bytes 90112 | tf_op jit(solution)/shard_map/concatenate | solution.py:541
  1.8 68.2 %layer.1 = bf16[64,1536]{1,0:T(8,128)(2,1)} custom-call(s32[2,2]{1,0:T(2,128)} %spans_ref.1, s32[2,256]{1,0:T(2,128)} %rec_ref.1, f32[64,128]{1,0:T(8,128)} %get-tuple-element.8.cos_ref, f32[64,128]{1,0:T(8,128)} %get-tuple-element.9.sin_ref, bf16[2,32,1536]{2,1,0:T(8,128)(2,1)} %q_ref.1, bf16[2,2,32,512]{3,2,1,0:T(8,128)(2,1)} %new_ref.1, ...), custom_call_target="tpu_custom_call" | custom-call | tf_op jit(solution)/shard_map/layer/pallas_call | solution.py:548
  70.0 1.6 %copy.14 = bf16[2,32,1536]{2,1,0:T(8,128)(2,1)} copy(bf16[2,32,1536]{2,1,0:T(8,128)(2,1)} %bitcast.4) | data formatting | bytes 393216
  (1 shorter events, 0.0 us)

commit v4 on v3

--- a/solution.py
+++ b/solution.py
@@ -301,8 +301,11 @@
         pltpu.roll(fresh, fresh.shape[1] - HD // 2, 1),
         pltpu.roll(fresh, HD // 2, 1),
     )
-    fresh = fresh * jnp.tile(cos_ref[...], (1, KVH // 2)) + partner * jnp.tile(
-        sin_ref[...], (1, KVH // 2)
+    cosine, sine = cos_ref[...], sin_ref[...]
+    cos_table = jnp.concatenate([cosine] * 4, axis=1)
+    sin_table = jnp.concatenate([-sine, sine, -sine, sine], axis=1)
+    fresh = fresh * jnp.tile(cos_table, (1, KVH // 2)) + partner * jnp.tile(
+        sin_table, (1, KVH // 2)
     )
     for h in range(KVH):
         cols = slice((h // 2) * 2 * HD, (h // 2 + 1) * 2 * HD)
@@ -481,7 +484,7 @@
 
         lax.fori_loop(0, local_experts, expert, 0)
         psend[r] = total[...].astype(bf16).reshape(N, tok, width)
-        for k in range(1, N):
+        for k in sorted(range(1, N), key=lambda k: abs(2 * k - N)):
             back_copy(r, k, mz).start()
     for r in range(2):
         rows = slice(r * tok, (r + 1) * tok)
@@ -538,8 +541,6 @@
     inverse = THETA ** (-(jnp.arange(half).astype(f32) * (2.0 / HD)))
     angles = positions.reshape(req_rows * held, 1).astype(f32) * inverse
     cosine, sine = jnp.cos(angles), jnp.sin(angles)
-    cos_table = jnp.concatenate([cosine] * 4, axis=1)
-    sin_table = jnp.concatenate([-sine, sine, -sine, sine], axis=1)
     vmem = pl.BlockSpec(memory_space=pltpu.VMEM)
     smem = pl.BlockSpec(memory_space=pltpu.SMEM)
     hbm = pl.BlockSpec(memory_space=pl.ANY)
@@ -586,8 +587,8 @@
     )(
         cache_spans,
         recompute_rows,
-        cos_table,
-        sin_table,
+        cosine,
+        sine,
         queries,
         new_kv,
         cache_kv,

time: 72.9 us -> 72.8 us (level)
    sin x0 -> x1, other arithmetic: none -> 0.83 us  [head_parallel_body(): cosine, sine = (jnp.cos(angles), jnp.sin(angles))]
    concatenate x1 -> x0, other arithmetic: 0.74 us -> none  [head_parallel_body(): cos_table = jnp.concatenate([cosine] * 4, axis=1)]
where the time goes in v4:
time: 72.8 us; the launch traced here: 71.5 us
  Pallas kernels  68.2 us (94%)
  local copies, waits for them, and re-layouts  1.7 us (2%)
  other arithmetic  1.59 us (2%)
    pallas_call x1, Pallas kernels, head_parallel_body(): pl.pallas_call(layer_kernel, out_shape=jax.ShapeDtypeStruct((rows, width)...  68.2 us
    unnamed x1, local copies, waits for them, and re-layouts  1.62 us

profile of v4, /device:TPU:2, one launch (start us, length us, event | category | flops | bytes accessed | tf_op | source)
XLA Modules:
  0.0 71.5 jit_solution(544252626520049258)
XLA Ops:
  0.0 0.8 %dynamic-slice_convert_fusion = f32[2,32]{1,0:T(2,128)S(1)} fusion(s32[2,256]{1,0:T(2,128)} %rec_ref.1, s32[]{:T(128)S(6)} %select_n.3), kind=kLoop, calls=%fused_computation.2 | loop fusion | flops 64 | bytes 516 | tf_op jit(solution)/shard_map/convert_element_type | solution.py:542
  0.8 0.1 convert_element_type.19
  0.8 0.8 %multiply_sine_fusion = (f32[64,32]{1,0:T(8,128)}, f32[64,32]{1,0:T(8,128)}) fusion(f32[32]{0:T(128)S(1)} %negate_power_fusion, f32[64]{0:T(128)S(1)} %convert_element_type.19), kind=kLoop, calls=%fused_computation | loop fusion | flops 2048 | bytes 16768 | tf_op jit(solution)/shard_map/sin | solution.py:543
  1.7 68.2 %layer.1 = bf16[64,1536]{1,0:T(8,128)(2,1)} custom-call(s32[2,2]{1,0:T(2,128)} %spans_ref.1, s32[2,256]{1,0:T(2,128)} %rec_ref.1, f32[64,32]{1,0:T(8,128)} %get-tuple-element.6.cos_ref, f32[64,32]{1,0:T(8,128)} %get-tuple-element.5.sin_ref, bf16[2,32,1536]{2,1,0:T(8,128)(2,1)} %q_ref.1, bf16[2,2,32,512]{3,2,1,0:T(8,128)(2,1)} %new_ref.1, ...), custom_call_target="tpu_custom_call" | custom-call | tf_op jit(solution)/shard_map/layer/pallas_call | solution.py:549
  69.9 1.6 %copy.14 = bf16[2,32,1536]{2,1,0:T(8,128)(2,1)} copy(bf16[2,32,1536]{2,1,0:T(8,128)(2,1)} %bitcast.4) | data formatting | bytes 393216
  (1 shorter events, 0.0 us)
